TPU v7x, 32 devices: a whole 2x2x4 slice. The times are simulated.
32 devices in a mesh: sub: 16 (over z, y, x), node: 2 (over core).
Axes of the slice: x: 2, y: 2, z: 4, core: 2. Of those that a mesh axis runs over, the one named last changes fastest.
Arguments:
- search_vectors: float32 [16384, 256], P('sub'), may hold values from -60 to 60
- ritz_values: float32 [256], replicated, may hold values from -0.9 to 0.9
- matrix_blocks: float32 [128, 4, 128, 128], P('sub'), may hold values from -0.25 to 0.25
- block_lists: int32 [128, 4], P('sub'), may hold values from 0 to 127, as said below
- inverses: float32 [4, 2, 128, 128, 128], P('node', None, 'sub'), may hold values from -0.5 to 0.5
- panels: float32 [16, 512, 1024], P('sub'), may hold values from -0.1875 to 0.1875
- separator_map: int32 [16, 4], P('sub'), may hold values from 0 to 7, as said below
- separator_shift: float32 [1024], replicated, may hold values from -0.9 to 0.9
Outputs:
- normalized_vectors: float32 [16384, 256], P('sub', 'node')
Inputs may be any that keep to these rules, and one draw needn't show every extreme that they name: `block_lists`: entry 0 of row g is g; the other entries of row g are distinct blocks from g - 4 to g + 4, none equal to g. `separator_map`: the entries of one row are distinct.
All inputs are finite; a program needn't handle non-finite values.
Results may differ from a plain program's by a relative error of at most 0.0001.
Values sent between devices are 32-bit elements; how exact they have to be, the bound alone decides.
A program may use at most 64 MiB of HBM per device.

v0:
```python
import math
import jax
import jax.numpy as jnp
from jax import lax
from jax.sharding import PartitionSpec as P

HALO_BLOCKS = 4
SEP_GROUPS = 8
HIGHEST = lax.Precision.HIGHEST


def with_halo(shard, sides, width):
    for axis, dim in sides:
        size, length = (lax.axis_size(axis), shard.shape[dim])
        up = [(i, (i + 1) % size) for i in range(size - 1)]
        down = [(j, i) for i, j in up]
        last = lax.slice_in_dim(shard, length - width, length, axis=dim)
        first = lax.slice_in_dim(shard, 0, width, axis=dim)
        before = lax.ppermute(last, axis, up)
        after = lax.ppermute(first, axis, down)
        shard = jnp.concatenate([before, shard, after], axis=dim)
    return shard


def scale_coarse(summed, shift_rows, real_shift, imag_shift):
    real_gap = real_shift[:, None, None] - shift_rows[None, :, None]
    imag_gap = imag_shift[:, None, None]
    modulus = real_gap * real_gap + imag_gap * imag_gap
    real_part = summed[:, 0]
    imag_part = summed[:, 1]
    return jnp.stack(
        [
            (real_part * real_gap + imag_part * imag_gap) / modulus,
            (imag_part * real_gap - real_part * imag_gap) / modulus,
        ],
        axis=1,
    )


def shards(
    search_vectors,
    ritz_values,
    matrix_blocks,
    block_lists,
    inverses,
    panels,
    separator_map,
    separator_shift,
):
    row_count, width = search_vectors.shape
    block_count, degree_count, block_size, _ = matrix_blocks.shape
    node_count = lax.axis_size("node")
    col_count = width // node_count
    node_index = lax.axis_index("node")
    sub_index = lax.axis_index("sub")
    column_start = node_index * col_count
    local_index = block_lists - sub_index * block_count + HALO_BLOCKS
    own_columns = lax.dynamic_slice_in_dim(search_vectors, column_start, col_count, 1)
    own_ritz = lax.dynamic_slice_in_dim(ritz_values, column_start, col_count, 0)
    padded = with_halo(own_columns, (("sub", 0),), HALO_BLOCKS * block_size)
    picked = padded.reshape(block_count + 2 * HALO_BLOCKS, block_size, -1)[local_index]
    local_part = (
        jnp.einsum("bkij,bkjm->bim", matrix_blocks, picked, precision=HIGHEST).reshape(
            row_count, -1
        )
        - own_columns * own_ritz[None, :]
    )
    residual = lax.all_gather(local_part, "node", axis=1, tiled=True)
    node_local = inverses.shape[0]
    total_nodes = node_local * node_count
    node_ids = (node_index * node_local + jnp.arange(node_local, dtype=jnp.int32)).astype(
        jnp.float32
    )
    angles = math.pi * (node_ids + 0.5) / total_nodes
    real_shift = jnp.cos(angles)
    imag_shift = jnp.sin(angles)
    res_blocks = residual.reshape(block_count, block_size, width)
    first_guess = jnp.einsum("ncbij,bjm->ncbim", inverses, res_blocks, precision=HIGHEST).reshape(
        node_local, 2, row_count, width
    )
    my_panel = panels[0]
    sep_count = my_panel.shape[0] // block_size
    partial_value = jnp.einsum("sr,ncrm->ncsm", my_panel, first_guess, precision=HIGHEST)
    one_hot = (
        separator_map[0][:, None] == jnp.arange(SEP_GROUPS, dtype=jnp.int32)[None, :]
    ).astype(jnp.float32)
    spread = jnp.einsum(
        "pg,ncpkm->ncgkm",
        one_hot,
        partial_value.reshape(node_local, 2, sep_count, block_size, width),
        precision=HIGHEST,
    ).reshape(node_local, 2, SEP_GROUPS * block_size, width)
    summed_all = lax.psum(spread, "sub")
    scaled = scale_coarse(summed_all, separator_shift, real_shift, imag_shift)
    picked_back = jnp.einsum(
        "pg,ncgkm->ncpkm",
        one_hot,
        scaled.reshape(node_local, 2, SEP_GROUPS, block_size, width),
        precision=HIGHEST,
    ).reshape(node_local, 2, sep_count * block_size, width)
    spread_back = jnp.einsum("sr,ncsm->ncrm", my_panel, picked_back, precision=HIGHEST).reshape(
        node_local, 2, block_count, block_size, width
    )
    products = jnp.einsum("ncbij,ndbjm->ncdbim", inverses, spread_back, precision=HIGHEST).reshape(
        node_local, 2, 2, row_count, width
    )
    sol_real = first_guess[:, 0] - (products[:, 0, 0] - products[:, 1, 1])
    sol_imag = first_guess[:, 1] - (products[:, 0, 1] + products[:, 1, 0])
    weight_real = 2.0 / total_nodes * real_shift
    weight_imag = 2.0 / total_nodes * imag_shift
    weighted = jnp.sum(
        weight_real[:, None, None] * sol_real - weight_imag[:, None, None] * sol_imag, axis=0
    )
    node_total = lax.psum_scatter(weighted, "node", scatter_dimension=1, tiled=True)
    updated = lax.dynamic_slice_in_dim(search_vectors, column_start, col_count, 1) - node_total
    squares = lax.psum(jnp.sum(updated * updated, axis=0), "sub")
    total_rows = row_count * lax.axis_size("sub")
    return updated * lax.rsqrt(squares / total_rows + 1e-06)[None, :]


def solution(mesh):
    return jax.shard_map(
        shards,
        mesh=mesh,
        in_specs=(
            P("sub", None),
            P(),
            P("sub", None, None, None),
            P("sub", None),
            P("node", None, "sub", None, None),
            P("sub", None, None),
            P("sub", None),
            P(),
        ),
        out_specs=P("sub", "node"),
        check_vma=False,
    )
```

profile of v0, /device:TPU:0, one launch (start us, length us, event | category | flops | bytes accessed | tf_op | source)
XLA Modules:
  0.0 344.4 jit_solution(13921328892674392484)
XLA Ops:
  7.8 4.9 %collective-permute-start = (f32[512,128]{1,0:T(8,128)S(1)}, f32[512,128]{1,0:T(8,128)S(1)}, u32[]{:S(2)}, u32[]{:S(2)}) collective-permute-start(f32[512,128]{1,0:T(8,128)S(1)} %get-tuple-element.9), channel_id=1, source_target_pairs={{0,2},{2,4},{4,6},{6,8},{8,10},{10,12},{12,14},{14,16},{16,18},{18... | collective-permute-start | bytes 786440 | tf_op jit(solution)/shard_map/ppermute | solution.py:19
  16.6 7.2 %collective-permute-done = f32[512,128]{1,0:T(8,128)S(1)} collective-permute-done((f32[512,128]{1,0:T(8,128)S(1)}, f32[512,128]{1,0:T(8,128)S(1)}, u32[]{:S(2)}, u32[]{:S(2)}) %collective-permute-start) | collective-permute-done | bytes 262176 | tf_op jit(solution)/shard_map/ppermute | solution.py:19
  23.8 2.0 collective-permute-done.1
  26.9 2.0 gather_fusion
  28.9 4.7 %fusion.41 = f32[8,128,128,1]{1,2,3,0:T(8,128)S(1)} fusion(f32[8,4,128,128]{3,2,1,0:T(8,128)} %bitcast.141, f32[8,4,128,128]{3,2,1,0:T(8,128)} %param.10), kind=kOutput, calls=%fused_computation.59 | convolution fusion | flops 805306368 | bytes 4718592 | tf_op jit(solution)/shard_map/bkij,bkjm->bim/dot_general | solution.py:63
  34.7 9.0 %all-gather.2.cloned.1.call-done = f32[1024,256]{1,0:T(8,128)} async-done(((f32[1024,128]{1,0:T(8,128)}), f32[1024,256]{1,0:T(8,128)}) %all-gather.2.cloned.1.call-update) | async-done | bytes 1048592 | tf_op jit(solution)/shard_map/all_gather | solution.py:68
  43.7 4.7 %convolution_bitcast_fusion.1 = f32[2,2,8,128,256]{4,3,1,0,2:T(8,128)S(1)} fusion(f32[8,128,256,1,1]{2,1,4,3,0:T(8,128)} %bitcast.145, f32[2,2,8,128,128]{4,3,2,1,0:T(8,128)S(1)} %copy-done), kind=kOutput, calls=%fused_computation.9 | convolution fusion | flops 1610612736 | bytes 7340032 | tf_op jit(solution)/shard_map/ncbij,bjm->ncbim/dot_general | solution.py:78
  48.9 2.0 copy-done.1
  50.9 14.7 %fusion.25 = f32[2,2,512,256]{2,3,1,0:T(8,128)} fusion(f32[2,2,1024,256]{3,2,1,0:T(8,128)S(1)} %bitcast.134, f32[1,512,1024]{2,1,0:T(8,128)S(1)} %copy-done.3), kind=kOutput, calls=%fused_computation.34 | convolution fusion | flops 6442450944 | bytes 8388608 | tf_op jit(solution)/shard_map/sr,ncrm->ncsm/dot_general | solution.py:83
  65.6 2.9 reshape.134
  68.5 4.1 %copy.20 = f32[2,2,4,128,256]{4,2,3,1,0:T(4,128)} copy(f32[2,2,4,128,256]{3,2,4,1,0:T(4,128)} %reshape.134) | data formatting | bytes 4194304 | tf_op jit(solution)/shard_map/reshape | solution.py:90
  72.6 3.8 %convolution_bitcast_fusion = f32[2,2,8,128,256]{4,2,3,1,0:T(8,128)S(1)} fusion(f32[2,2,4,128,256]{4,2,3,1,0:T(4,128)} %copy.20, s32[4]{0:T(128)S(1)} %bitcast.146), kind=kOutput, calls=%fused_computation.8 | convolution fusion | flops 50331680 | bytes 6291472 | tf_op jit(solution)/shard_map/pg,ncpkm->ncgkm/dot_general | solution.py:87
  76.4 3.3 copy.21
  80.4 169.0 %all-reduce.2.cloned.1.call-done = f32[2,2,1024,256]{3,2,1,0:T(8,128)} async-done(((f32[2,2,1024,256]{3,2,1,0:T(8,128)}), f32[2,2,1024,256]{3,2,1,0:T(8,128)}) %all-reduce.2.cloned.1.call-update) | async-done | bytes 4194320 | tf_op jit(solution)/shard_map/psum | solution.py:93
  249.4 3.0 add_divide_fusion
  254.8 2.1 fusion.28
  258.5 7.0 %fusion.19 = f32[2,2,256,1024]{3,2,1,0:T(8,128)S(1)} fusion(f32[2,2,512,256]{3,2,1,0:T(8,128)S(1)} %bitcast.144, f32[1,512,1024]{2,1,0:T(8,128)S(1)} %copy-done.4), kind=kOutput, calls=%fused_computation.26 | convolution fusion | flops 6442450944 | bytes 8388608 | tf_op jit(solution)/shard_map/sr,ncsm->ncrm/dot_general | solution.py:101
  266.7 7.8 %fusion.6 = f32[2,2,2,8,128,256]{5,4,1,2,3,0:T(8,128)S(1)} fusion(f32[2,2,8,128,256,1]{3,2,4,1,0,5:T(8,128)S(1)} %bitcast.137, f32[2,2,8,128,128]{4,3,2,1,0:T(8,128)S(1)} %copy-done), kind=kOutput, calls=%fused_computation.7 | convolution fusion | flops 3221225472 | bytes 14680064 | tf_op jit(solution)/shard_map/ncbij,ndbjm->ncdbim/dot_general | solution.py:104
  274.5 4.2 %copy.28 = f32[2,2,2,8,128,256]{5,4,3,2,1,0:T(8,128)} copy(f32[2,2,2,8,128,256]{5,4,1,2,3,0:T(8,128)S(1)} %fusion.6) | data formatting | bytes 16777216 | tf_op jit(solution)/shard_map/ncbij,ndbjm->ncdbim/transpose | solution.py:104
  278.7 5.6 %fusion.14 = f32[1024,256]{1,0:T(8,128)} fusion(f32[2,2,2,1024,256]{4,3,2,1,0:T(8,128)} %bitcast.136, f32[2,2,1024,256]{3,2,1,0:T(8,128)S(1)} %bitcast.135, f32[2]{0:T(128)S(1)} %get-tuple-element.13, f32[2]{0:T(128)S(1)} %get-tuple-element.14), kind=kLoop, calls=%fused_computation.16 | loop fusion | flops 3932160 | bytes 13631504 | tf_op jit(solution)/shard_map/reduce_sum | solution.py:111
  284.3 7.6 %reduce-scatter.2.cloned.1.call-done = f32[1024,128]{1,0:T(8,128)} async-done(((f32[1024,256]{1,0:T(8,128)}), f32[1024,128]{1,0:T(8,128)}) %reduce-scatter.2.cloned.1.call-update) | async-done | bytes 524304 | tf_op jit(solution)/shard_map/reduce_scatter | solution.py:114
  291.9 1.9 multiply_reduce_fusion
  293.8 42.0 %psum.15 = f32[128]{0:T(128)S(1)} all-reduce(f32[128]{0:T(128)S(1)} %get-tuple-element.5), channel_id=1, replica_groups=mesh['sub'=16,'node'=2] {'sub'}, use_global_device_ids=true, to_apply=%region_4.0 | all-reduce | flops 128 | bytes 1024 | tf_op jit(solution)/shard_map/psum | solution.py:116
  335.8 1.9 broadcast_multiply_fusion
  (41 shorter events, 13.7 us)
Async XLA Ops:
  6.5 37.2 %copy-start = (f32[2,2,8,128,128]{4,3,2,1,0:T(8,128)S(1)}, f32[2,2,8,128,128]{4,3,2,1,0:T(8,128)}, u32[]{:S(2)}) copy-start(f32[2,2,8,128,128]{4,3,2,1,0:T(8,128)} %param.12) | copy-start | bytes 6291460
  6.5 37.2 %all-gather.2.cloned.1.call-start = ((), (), s32[]{:S(2)}) async-start(), calls=%async_computation.1 | async-start | bytes 1572864 | tf_op jit(solution)/shard_map/all_gather | solution.py:68
  7.8 16.1 %collective-permute-start = (f32[512,128]{1,0:T(8,128)S(1)}, f32[512,128]{1,0:T(8,128)S(1)}, u32[]{:S(2)}, u32[]{:S(2)}) collective-permute-start(f32[512,128]{1,0:T(8,128)S(1)} %get-tuple-element.9), channel_id=1, source_target_pairs={{0,2},{2,4},{4,6},{6,8},{8,10},{10,12},{12,14},{14,16},{16,18},{18... | collective-permute-start | bytes 786440 | tf_op jit(solution)/shard_map/ppermute | solution.py:19
  12.7 13.2 %collective-permute-start.1 = (f32[512,128]{1,0:T(8,128)S(1)}, f32[512,128]{1,0:T(8,128)}, u32[]{:S(2)}, u32[]{:S(2)}) collective-permute-start(f32[512,128]{1,0:T(8,128)S(1)} %get-tuple-element.10), channel_id=1, source_target_pairs={{2,0},{4,2},{6,4},{8,6},{10,8},{12,10},{14,12},{16,14},{18,16},{20... | collective-permute-start | bytes 786440 | tf_op jit(solution)/shard_map/ppermute | solution.py:20
  28.9 4.7 %copy-start.5 = (f32[1024,256]{1,0:T(8,128)S(1)}, f32[1024,256]{1,0:T(8,128)}, u32[]{:S(2)}) copy-start(f32[1024,256]{1,0:T(8,128)} %param.8) | copy-start | bytes 3145732
  34.5 214.9 %all-reduce.2.cloned.1.call-start = ((), (), s32[]{:S(2)}) async-start(), calls=%async_computation.2 | async-start | bytes 8388608 | tf_op jit(solution)/shard_map/psum | solution.py:93
  48.5 2.4 copy-start.3
  48.9 2.0 copy-start.1
  68.5 4.1 %copy-start.7 = (s32[1,4]{1,0:T(1,128)S(1)}, s32[1,4]{1,0:T(1,128)}, u32[]{:S(2)}) copy-start(s32[1,4]{1,0:T(1,128)} %param.14) | copy-start | bytes 52
  79.7 0.7 copy-start.6
  79.7 212.2 %reduce-scatter.2.cloned.1.call-start = ((), (), s32[]{:S(2)}) async-start(), calls=%async_computation.3 | async-start | bytes 1572864 | tf_op jit(solution)/shard_map/reduce_scatter | solution.py:114
  256.9 1.6 copy-start.4
  274.5 4.2 %copy-start.2 = (f32[2,2,8,128,256]{4,3,2,1,0:T(8,128)S(1)}, f32[2,2,8,128,256]{4,3,2,1,0:T(8,128)}, u32[]{:S(2)}) copy-start(f32[2,2,8,128,256]{4,3,2,1,0:T(8,128)} %copy-done.1) | copy-start | bytes 12582916
Sparse Core Ops, SparseCore 0:
  34.6 9.0 all-gather.1
  79.8 169.5 all-reduce.1
  284.4 7.4 reduce-scatter.1
where the time goes:
time: 348 us; the launch traced here: 344 us
  waiting for transfers between devices  195 us (56%)
  matrix products  44.8 us (13%)
  blocking collectives  42 us (12%)
  local copies, waits for them, and re-layouts  27.8 us (8%)
  other arithmetic  15.1 us (4%)
  between operations  13.5 us (4%)
  starting transfers between devices  6.44 us (2%)
    psum x1, waiting for transfers between devices, shards(): summed_all = lax.psum(spread, 'sub')  169 us
    psum x1, blocking collectives, shards(): squares = lax.psum(jnp.sum(updated * updated, axis=0), 'sub')  42 us
    dot_general x1, matrix products, shards(): jnp.einsum('sr,ncrm->ncsm', my_panel, first_guess, precision=HIGHEST)  14.7 us
    all_gather x1, waiting for transfers between devices, shards(): residual = lax.all_gather(local_part, 'node', axis=1, tiled=True)  9.01 us
    dot_general x1, matrix products, shards(): jnp.einsum('ncbij,ndbjm->ncdbim', inverses, spread_back, precision=HIGHEST)  7.8 us
    reduce_scatter x1, waiting for transfers between devices, shards(): lax.psum_scatter(weighted, 'node', scatter_dimension=1, tiled=True)  7.57 us
    ppermute x1, waiting for transfers between devices, with_halo(): before = lax.ppermute(last, axis, up)  7.18 us
    reshape x2, local copies, waits for them, and re-layouts, shards(): partial_value.reshape(node_local, 2, sep_count, block_size, width)  7.06 us
  transfers between devices with their start and end apart: 5, of which 5 were waited for; matrix products, arithmetic and copies ran while one was open for 1% of the time, Pallas kernels for 0%

commit v1 on v0

--- a/solution.py
+++ b/solution.py
@@ -90,7 +90,11 @@
         partial_value.reshape(node_local, 2, sep_count, block_size, width),
         precision=HIGHEST,
     ).reshape(node_local, 2, SEP_GROUPS * block_size, width)
-    summed_all = lax.psum(spread, "sub")
+    summed_all = spread
+    for hop in (1, 2, 4, 8):
+        summed_all = summed_all + lax.ppermute(
+            summed_all, "sub", [(dev, dev ^ hop) for dev in range(16)]
+        )
     scaled = scale_coarse(summed_all, separator_shift, real_shift, imag_shift)
     picked_back = jnp.einsum(
         "pg,ncgkm->ncpkm",

time: 348 us -> 642 us (1.84)
  waiting for transfers between devices: 195 us -> 477 us
  starting transfers between devices: 6.44 us -> 14.5 us
    ppermute x0 -> x4, waiting for transfers between devices: none -> 449 us  [shards(): lax.ppermute(summed_all, 'sub', [(dev, dev ^ hop) for dev in range(16)])]
    psum x1 -> x0, waiting for transfers between devices: 169 us -> none  [shards(): summed_all = lax.psum(spread, 'sub')]
    add x0 -> x4, other arithmetic: none -> 8.11 us  [shards(): summed_all + lax.ppermute(summed_all, 'sub', [(dev, dev ^ hop) for dev in...]
    ppermute x0 -> x4, starting transfers between devices: none -> 8.08 us  [shards(): lax.ppermute(summed_all, 'sub', [(dev, dev ^ hop) for dev in range(16)])]
  transfers between devices with their start and end apart: 5 -> 8, of which waited for: 5 -> 8; matrix products, arithmetic and copies ran while one was open for 1% -> 0% of each run, Pallas kernels for 0% -> 0%
where the time goes in v1:
time: 642 us; the launch traced here: 639 us
  waiting for transfers between devices  477 us (74%)
  matrix products  45 us (7%)
  blocking collectives  41.9 us (7%)
  local copies, waits for them, and re-layouts  25.4 us (4%)
  other arithmetic  21.2 us (3%)
  starting transfers between devices  14.5 us (2%)
  between operations  13.8 us (2%)
    ppermute x4, waiting for transfers between devices, shards(): lax.ppermute(summed_all, 'sub', [(dev, dev ^ hop) for dev in range(16)])  449 us
    psum x1, blocking collectives, shards(): squares = lax.psum(jnp.sum(updated * updated, axis=0), 'sub')  41.9 us
    dot_general x1, matrix products, shards(): jnp.einsum('sr,ncrm->ncsm', my_panel, first_guess, precision=HIGHEST)  14.9 us
  transfers between devices with their start and end apart: 8, of which 8 were waited for; matrix products, arithmetic and copies ran while one was open for 0% of the time, Pallas kernels for 0%

profile of v1, /device:TPU:0, one launch (start us, length us, event | category | flops | bytes accessed | tf_op | source)
XLA Modules:
  0.0 638.6 jit_solution(4236765382701957985)
XLA Ops:
  7.8 4.9 collective-permute-start
  16.6 7.2 %collective-permute-done = f32[512,128]{1,0:T(8,128)S(1)} collective-permute-done((f32[512,128]{1,0:T(8,128)S(1)}, f32[512,128]{1,0:T(8,128)S(1)}, u32[]{:S(2)}, u32[]{:S(2)}) %collective-permute-start) | collective-permute-done | bytes 262176 | tf_op jit(solution)/shard_map/ppermute | solution.py:19
  26.9 2.0 gather_fusion
  28.9 4.7 fusion.41
  34.7 9.0 %all-gather.2.cloned.1.call-done = f32[1024,256]{1,0:T(8,128)} async-done(((f32[1024,128]{1,0:T(8,128)}), f32[1024,256]{1,0:T(8,128)}) %all-gather.2.cloned.1.call-update) | async-done | bytes 1048592 | tf_op jit(solution)/shard_map/all_gather | solution.py:68
  43.7 4.7 convolution_bitcast_fusion.1
  50.9 14.9 %fusion.25 = f32[2,2,512,256]{2,3,1,0:T(8,128)} fusion(f32[2,2,1024,256]{3,2,1,0:T(8,128)S(1)} %bitcast.135, f32[1,512,1024]{2,1,0:T(8,128)S(1)} %copy-done.3), kind=kOutput, calls=%fused_computation.34 | convolution fusion | flops 6442450944 | bytes 8388608 | tf_op jit(solution)/shard_map/sr,ncrm->ncsm/dot_general | solution.py:83
  65.8 2.9 reshape.134
  68.7 4.1 copy.20
  72.8 3.8 convolution_bitcast_fusion
  79.7 91.0 %collective-permute-done.2 = f32[2,2,1024,256]{3,2,1,0:T(8,128)S(1)} collective-permute-done((f32[2,2,1024,256]{3,2,1,0:T(8,128)S(1)}, f32[2,2,1024,256]{3,2,1,0:T(8,128)S(1)}, u32[]{:S(2)}, u32[]{:S(2)}) %collective-permute-start.2) | collective-permute-done | bytes 4194336 | tf_op jit(solution)/shard_map/ppermute | solution.py:95
  173.6 90.2 %collective-permute-done.3 = f32[2,2,1024,256]{3,2,1,0:T(8,128)S(1)} collective-permute-done((f32[2,2,1024,256]{3,2,1,0:T(8,128)S(1)}, f32[2,2,1024,256]{3,2,1,0:T(8,128)S(1)}, u32[]{:S(2)}, u32[]{:S(2)}) %collective-permute-start.3) | collective-permute-done | bytes 4194336 | tf_op jit(solution)/shard_map/ppermute | solution.py:95
  266.1 89.3 %collective-permute-done.4 = f32[2,2,1024,256]{3,2,1,0:T(8,128)S(1)} collective-permute-done((f32[2,2,1024,256]{3,2,1,0:T(8,128)S(1)}, f32[2,2,1024,256]{3,2,1,0:T(8,128)S(1)}, u32[]{:S(2)}, u32[]{:S(2)}) %collective-permute-start.4) | collective-permute-done | bytes 4194336 | tf_op jit(solution)/shard_map/ppermute | solution.py:95
  355.4 2.5 add.115
  357.9 2.6 collective-permute-start.5
  360.8 178.4 %collective-permute-done.5 = f32[2,2,1024,256]{3,2,1,0:T(8,128)} collective-permute-done((f32[2,2,1024,256]{3,2,1,0:T(8,128)}, f32[2,2,1024,256]{3,2,1,0:T(8,128)}, u32[]{:S(2)}, u32[]{:S(2)}) %collective-permute-start.5) | collective-permute-done | bytes 4194336 | tf_op jit(solution)/shard_map/ppermute | solution.py:95
  539.2 4.0 add.116
  546.6 2.1 fusion.28
  550.3 7.0 %fusion.19 = f32[2,2,256,1024]{3,2,1,0:T(8,128)S(1)} fusion(f32[2,2,512,256]{3,2,1,0:T(8,128)S(1)} %bitcast.145, f32[1,512,1024]{2,1,0:T(8,128)S(1)} %copy-done.4), kind=kOutput, calls=%fused_computation.26 | convolution fusion | flops 6442450944 | bytes 8388608 | tf_op jit(solution)/shard_map/sr,ncsm->ncrm/dot_general | solution.py:105
  558.6 7.8 %fusion.6 = f32[2,2,2,8,128,256]{5,4,1,2,3,0:T(8,128)S(1)} fusion(f32[2,2,8,128,256,1]{3,2,4,1,0,5:T(8,128)S(1)} %bitcast.139, f32[2,2,8,128,128]{4,3,2,1,0:T(8,128)S(1)} %copy-done), kind=kOutput, calls=%fused_computation.7 | convolution fusion | flops 3221225472 | bytes 14680064 | tf_op jit(solution)/shard_map/ncbij,ndbjm->ncdbim/dot_general | solution.py:108
  566.4 4.2 copy.28
  570.5 5.6 fusion.14
  576.1 9.6 %reduce-scatter.2.cloned.1.call-done = f32[1024,128]{1,0:T(8,128)} async-done(((f32[1024,256]{1,0:T(8,128)}), f32[1024,128]{1,0:T(8,128)}) %reduce-scatter.2.cloned.1.call-update) | async-done | bytes 524304 | tf_op jit(solution)/shard_map/reduce_scatter | solution.py:118
  587.7 41.9 %psum.7 = f32[128]{0:T(128)S(1)} all-reduce(f32[128]{0:T(128)S(1)} %get-tuple-element.5), channel_id=1, replica_groups=mesh['sub'=16,'node'=2] {'sub'}, use_global_device_ids=true, to_apply=%region_3.0 | all-reduce | flops 128 | bytes 1024 | tf_op jit(solution)/shard_map/psum | solution.py:120
  (50 shorter events, 30.3 us)
Async XLA Ops:
  6.5 37.2 %copy-start = (f32[2,2,8,128,128]{4,3,2,1,0:T(8,128)S(1)}, f32[2,2,8,128,128]{4,3,2,1,0:T(8,128)}, u32[]{:S(2)}) copy-start(f32[2,2,8,128,128]{4,3,2,1,0:T(8,128)} %param.12) | copy-start | bytes 6291460
  6.5 37.2 %all-gather.2.cloned.1.call-start = ((), (), s32[]{:S(2)}) async-start(), calls=%async_computation.1 | async-start | bytes 1572864 | tf_op jit(solution)/shard_map/all_gather | solution.py:68
  7.8 16.1 %collective-permute-start = (f32[512,128]{1,0:T(8,128)S(1)}, f32[512,128]{1,0:T(8,128)S(1)}, u32[]{:S(2)}, u32[]{:S(2)}) collective-permute-start(f32[512,128]{1,0:T(8,128)S(1)} %get-tuple-element.9), channel_id=1, source_target_pairs={{0,2},{2,4},{4,6},{6,8},{8,10},{10,12},{12,14},{14,16},{16,18},{18... | collective-permute-start | bytes 786440 | tf_op jit(solution)/shard_map/ppermute | solution.py:19
  12.7 13.2 %collective-permute-start.1 = (f32[512,128]{1,0:T(8,128)S(1)}, f32[512,128]{1,0:T(8,128)}, u32[]{:S(2)}, u32[]{:S(2)}) collective-permute-start(f32[512,128]{1,0:T(8,128)S(1)} %get-tuple-element.10), channel_id=1, source_target_pairs={{2,0},{4,2},{6,4},{8,6},{10,8},{12,10},{14,12},{16,14},{18,16},{20... | collective-permute-start | bytes 786440 | tf_op jit(solution)/shard_map/ppermute | solution.py:20
  28.9 4.7 copy-start.5
  34.5 551.3 %reduce-scatter.2.cloned.1.call-start = ((), (), s32[]{:S(2)}) async-start(), calls=%async_computation.2 | async-start | bytes 1572864 | tf_op jit(solution)/shard_map/reduce_scatter | solution.py:118
  48.5 2.4 copy-start.3
  48.9 2.0 copy-start.1
  68.7 4.1 copy-start.7
  77.9 92.8 %collective-permute-start.2 = (f32[2,2,1024,256]{3,2,1,0:T(8,128)S(1)}, f32[2,2,1024,256]{3,2,1,0:T(8,128)S(1)}, u32[]{:S(2)}, u32[]{:S(2)}) collective-permute-start(f32[2,2,1024,256]{3,2,1,0:T(8,128)S(1)} %bitcast.138), channel_id=1, source_target_pairs={{0,2},{2,0},{4,6},{6,4},{8,10},{10,8},{12,14},{14,12},{16,18},{18,... | collective-permute-start | bytes 12582920 | tf_op jit(solution)/shard_map/ppermute | solution.py:95
  171.8 92.0 %collective-permute-start.3 = (f32[2,2,1024,256]{3,2,1,0:T(8,128)S(1)}, f32[2,2,1024,256]{3,2,1,0:T(8,128)S(1)}, u32[]{:S(2)}, u32[]{:S(2)}) collective-permute-start(f32[2,2,1024,256]{3,2,1,0:T(8,128)S(1)} %bitcast_add_fusion), channel_id=1, source_target_pairs={{0,4},{2,6},{4,0},{6,2},{8,12},{10,14},{12,8},{14,10},{16,20},{18,... | collective-permute-start | bytes 12582920 | tf_op jit(solution)/shard_map/ppermute | solution.py:95
  264.3 96.4 %copy-start.6 = (f32[1024]{0:T(1024)S(1)}, f32[1024]{0:T(1024)}, u32[]{:S(2)}) copy-start(f32[1024]{0:T(1024)} %param.15) | copy-start | bytes 12292
  264.3 91.1 %collective-permute-start.4 = (f32[2,2,1024,256]{3,2,1,0:T(8,128)S(1)}, f32[2,2,1024,256]{3,2,1,0:T(8,128)S(1)}, u32[]{:S(2)}, u32[]{:S(2)}) collective-permute-start(f32[2,2,1024,256]{3,2,1,0:T(8,128)S(1)} %add.114), channel_id=1, source_target_pairs={{0,8},{2,10},{4,12},{6,14},{8,0},{10,2},{12,4},{14,6},{16,24},{18,... | collective-permute-start | bytes 12582920 | tf_op jit(solution)/shard_map/ppermute | solution.py:95
  357.9 181.3 %collective-permute-start.5 = (f32[2,2,1024,256]{3,2,1,0:T(8,128)}, f32[2,2,1024,256]{3,2,1,0:T(8,128)}, u32[]{:S(2)}, u32[]{:S(2)}) collective-permute-start(f32[2,2,1024,256]{3,2,1,0:T(8,128)} %add.115), channel_id=1, source_target_pairs={{0,16},{2,18},{4,20},{6,22},{8,24},{10,26},{12,28},{14,30},{16,0},... | collective-permute-start | bytes 12582920 | tf_op jit(solution)/shard_map/ppermute | solution.py:95
  548.7 1.6 copy-start.4
  566.4 4.2 copy-start.2
Sparse Core Ops, SparseCore 0:
  34.6 9.0 all-gather.1
  576.3 9.4 reduce-scatter.1
